TPU v7x, 32 devices: a whole 2x2x4 slice. The times are simulated.
32 devices in a mesh: front: 2 (over core), row: 4 (over y, x), col: 4 (over z).
Axes of the slice: x: 2, y: 2, z: 4, core: 2. Of those that a mesh axis runs over, the one named last changes fastest.
Arguments:
- child_blocks: bfloat16 [16384, 8192], P(('front', 'row'), 'col'), may hold values from -0.0625 to 0.0625
- sketch: bfloat16 [8192, 512], P('col'), may hold values from -6 to 6
- block_map: int32 [2, 64], P('front'), may hold values from 0 to 95, as said below
Outputs:
- parent_basis: float32 [512, 12288], P('col', ('front', 'row'))
Inputs may be any that keep to these rules, and one draw needn't show every extreme that they name: `block_map`: each row lists 8192 / 128 different parent blocks in increasing order.
All inputs are finite; a program needn't handle non-finite values.
Results may differ from a plain program's by a relative error of at most 0.0003.
Values sent between devices are 32-bit elements; how exact they have to be, the bound alone decides.
No kernel may reach another device: no remote copies, remote signals or barrier semaphores. Data moves between devices by JAX's collectives and lax.ppermute only.
A program may use at most 128 MiB of HBM per device.

v0:
```python
import jax
import jax.numpy as jnp
from jax import lax
from jax.sharding import PartitionSpec as P

P_SIZE = 12288
BLK = 128


def from_partner(array, axis, stride):
    return lax.ppermute(array, axis, [(i, i ^ 1 << stride) for i in range(lax.axis_size(axis))])


def shards(child_blocks, sketch, block_map):
    siblings = min(4, lax.axis_size("front"))
    levels = siblings.bit_length() - 1
    front_here = lax.axis_index("front")
    row_here = lax.axis_index("row")
    row_count = lax.axis_size("row")
    sketch_part = lax.psum_scatter(
        lax.dot_general(
            sketch, child_blocks, (((0,), (1,)), ((), ())), preferred_element_type=jnp.float32
        ),
        "col",
        scatter_dimension=0,
        tiled=True,
    )
    width_here = sketch_part.shape[0]
    parent_blocks = P_SIZE // BLK
    share_blocks = parent_blocks // (siblings * row_count)
    rows_all = lax.all_gather(sketch_part, "row", axis=1, tiled=True)
    maps_all = block_map[0]
    block_count = maps_all.shape[0]
    capacity = min(share_blocks, block_count)
    blocks_all = rows_all.reshape(width_here, block_count, BLK)
    dest_share = maps_all // share_blocks
    dest_sibling = dest_share // row_count
    dest_row = dest_share % row_count
    place_plus = (maps_all % share_blocks + 1).astype(jnp.float32)
    sibling_here = front_here % siblings
    slot_ids = jnp.arange(capacity, dtype=jnp.int32)
    place_ids = jnp.arange(share_blocks, dtype=jnp.int32).astype(jnp.float32)
    share = jnp.zeros((width_here, share_blocks, BLK), jnp.float32)
    for offset_bits in range(siblings):
        target_sibling = jnp.bitwise_xor(sibling_here, offset_bits)
        wanted = (dest_sibling == target_sibling) & (dest_row == row_here)
        slot = jnp.cumsum(wanted.astype(jnp.int32)) - 1
        select = (wanted[:, None] & (slot[:, None] == slot_ids[None, :])).astype(jnp.float32)
        packed = jnp.einsum("cbk,bj->cjk", blocks_all, select, precision=lax.Precision.HIGHEST)
        places = jnp.dot(place_plus, select, precision=lax.Precision.HIGHEST) - 1.0
        for bit_level in range(levels):
            if offset_bits >> bit_level & 1:
                packed, places = from_partner((packed, places), "front", bit_level)
        landing = (places[:, None] == place_ids[None, :]).astype(jnp.float32)
        share = share + jnp.einsum("cjk,jm->cmk", packed, landing, precision=lax.Precision.HIGHEST)
    share = share.reshape(width_here, share_blocks * BLK)
    columns_all = lax.all_gather(share, "col", axis=0, tiled=True)
    gram = lax.dot_general(
        columns_all, columns_all, (((1,), (1,)), ((), ())), precision=lax.Precision.HIGHEST
    )
    gram = lax.psum(gram, "row")
    for bit_level in range(levels):
        gram = gram + from_partner(gram, "front", bit_level)
    lower = jnp.linalg.cholesky(gram)
    basis = jax.scipy.linalg.solve_triangular(lower, columns_all, lower=True)
    return lax.dynamic_slice_in_dim(basis, lax.axis_index("col") * width_here, width_here, 0)


def solution(mesh):
    placed = (P(("front", "row"), "col"), P("col", None), P("front", None))
    return jax.shard_map(
        shards, mesh=mesh, in_specs=placed, out_specs=P("col", ("front", "row")), check_vma=False
    )
```

profile of v0, /device:TPU:0, one launch (start us, length us, event | category | flops | bytes accessed | tf_op | source)
XLA Modules:
  0.0 458.2 jit_solution(8747269671987431088)
XLA Ops:
  6.5 1.6 copy-done
  8.1 9.6 %fusion.80 = f32[512,2048]{1,0:T(8,128)} fusion(bf16[2048,512]{1,0:T(8,128)(2,1)S(1)} %copy-done, bf16[2048,2048]{1,0:T(8,128)(2,1)} %param.3), kind=kOutput, calls=%fused_computation.141 | convolution fusion | flops 4294967296 | bytes 14680064 | tf_op jit(solution)/shard_map/dot_general | solution.py:21
  17.8 79.6 %reduce-scatter.2.cloned.1.call-done = f32[128,2048]{1,0:T(8,128)} async-done(((f32[512,2048]{1,0:T(8,128)}), f32[128,2048]{1,0:T(8,128)}) %reduce-scatter.2.cloned.1.call-update) | async-done | bytes 1048592 | tf_op jit(solution)/shard_map/reduce_scatter | solution.py:20
  98.4 53.9 %all-gather.3.cloned.1.call-done = f32[128,8192]{1,0:T(8,128)} async-done(((f32[128,2048]{1,0:T(8,128)}), f32[128,8192]{1,0:T(8,128)}) %all-gather.3.cloned.1.call-update) | async-done | bytes 4194320 | tf_op jit(solution)/shard_map/all_gather | solution.py:31
  152.4 2.9 copy.25
  155.3 1.5 convolution_bitcast_fusion
  157.3 1.6 convolution_bitcast_fusion.1
  158.9 0.6 fusion.51
  159.5 1.0 fusion.8
  160.6 1.2 copy.20
  161.8 2.3 copy.21
  164.3 63.5 %all-gather.5.cloned.1.call-done = f32[512,1536]{1,0:T(8,128)} async-done(((f32[128,1536]{1,0:T(8,128)}), f32[512,1536]{1,0:T(8,128)}) %all-gather.5.cloned.1.call-update) | async-done | bytes 3145744 | tf_op jit(solution)/shard_map/all_gather | solution.py:57
  227.9 9.4 %fusion.81 = f32[512,512]{0,1:T(8,128)} fusion(f32[512,1536]{1,0:T(8,128)} %all-gather.5.cloned.1.call-done), kind=kOutput, calls=%fused_computation.142 | convolution fusion | flops 4831838208 | bytes 4194304 | tf_op jit(solution)/shard_map/dot_general | solution.py:58
  237.3 51.2 %all-reduce.3.cloned.1.call-done = f32[512,512]{0,1:T(8,128)} async-done(((f32[512,512]{0,1:T(8,128)}), f32[512,512]{0,1:T(8,128)}) %all-reduce.3.cloned.1.call-update) | async-done | bytes 1048592 | tf_op jit(solution)/shard_map/psum | solution.py:61
  288.5 3.0 collective-permute-done.2
  291.5 1.7 add.150
  293.3 1.3 copy.23
  294.6 1.4 fusion.11
  296.1 1.0 copy-done.2
  297.0 11.7 %cholesky.104 = f32[128,128]{1,0:T(8,128)S(1)} custom-call(f32[128,128]{1,0:T(8,128)S(1)} %cholesky.266), custom_call_target="Cholesky" | custom-call | tf_op jit(solution)/shard_map/jit(cholesky)/cholesky | solution.py:64
  308.9 9.8 %custom-call.31 = f32[1,128,128]{1,2,0:T(8,128)S(1)} custom-call(f32[1,128,128]{2,1,0:T(8,128)S(1)} %get-tuple-element.38), custom_call_target="InvertDiagBlocksLowerTriangular" | custom-call | tf_op jit(solution)/shard_map/jit(cholesky)/cholesky | solution.py:64
  318.7 1.2 constant_dynamic-update-slice_fusion
  320.0 1.3 slice_subtract_fusion
  321.3 11.7 %cholesky.217 = f32[128,128]{1,0:T(8,128)S(1)} custom-call(f32[128,128]{1,0:T(8,128)S(1)} %cholesky.270), custom_call_target="Cholesky" | custom-call | tf_op jit(solution)/shard_map/jit(cholesky)/cholesky | solution.py:64
  333.0 10.2 %custom-call.32 = f32[1,128,128]{1,2,0:T(8,128)S(1)} custom-call(f32[1,128,128]{2,1,0:T(8,128)S(1)} %get-tuple-element.35), custom_call_target="InvertDiagBlocksLowerTriangular" | custom-call | tf_op jit(solution)/shard_map/jit(cholesky)/cholesky | solution.py:64
  343.5 1.3 slice_subtract_fusion.1
  344.8 11.7 %cholesky.238 = f32[128,128]{1,0:T(8,128)S(1)} custom-call(f32[128,128]{1,0:T(8,128)S(1)} %cholesky.275), custom_call_target="Cholesky" | custom-call | tf_op jit(solution)/shard_map/jit(cholesky)/cholesky | solution.py:64
  356.5 9.8 %custom-call.33 = f32[1,128,128]{1,2,0:T(8,128)S(1)} custom-call(f32[1,128,128]{2,1,0:T(8,128)S(1)} %get-tuple-element.32), custom_call_target="InvertDiagBlocksLowerTriangular" | custom-call | tf_op jit(solution)/shard_map/jit(cholesky)/cholesky | solution.py:64
  366.5 1.2 slice_subtract_fusion.2
  367.8 11.9 %cholesky.255 = f32[128,128]{1,0:T(8,128)S(1)} custom-call(f32[128,128]{1,0:T(8,128)S(1)} %slice_subtract_fusion.2), custom_call_target="Cholesky" | custom-call | tf_op jit(solution)/shard_map/jit(cholesky)/cholesky | solution.py:64
  379.7 0.6 compare_reduce_fusion.1
  380.3 0.6 compare_reduce_fusion
  380.9 0.7 compare_reduce_fusion.2
  384.1 1.1 select_select_fusion
  385.2 13.8 %while.1 = (s32[]{:T(128)}, f32[512,512]{1,0:T(8,128)}, s32[4,2]{0,1:T(2,128)S(1)}, f32[4,128,128]{2,1,0:T(8,128)}, s32[]{:T(128)}) while((s32[]{:T(128)}, f32[512,512]{1,0:T(8,128)}, s32[4,2]{0,1:T(2,128)S(1)}, f32[4,128,128]{2,1,0:T(8,128)}, s32[]{:T(128)}) %tuple.31), condition=%wide.while_cond, body=%wide.while_body.sunk | while | flops 2 | bytes 132205 | solution.py:65
  385.8 2.9 bitcast_dynamic-update-slice_fusion.2
  389.3 2.9 bitcast_dynamic-update-slice_fusion.2
  392.7 2.9 bitcast_dynamic-update-slice_fusion.2
  396.2 2.8 bitcast_dynamic-update-slice_fusion.2
  399.0 40.1 %custom-call.34 = f32[4,128,128]{1,2,0:T(8,128)S(1)} custom-call(f32[4,128,128]{2,1,0:T(8,128)} %get-tuple-element.12), custom_call_target="InvertDiagBlocksLowerTriangular" | custom-call | tf_op jit(solution)/shard_map/jit(_solve_triangular)/triangular_solve | solution.py:65
  439.1 2.1 fusion.16
  441.3 2.0 convolution_subtract_fusion.2
  443.2 0.8 fusion.31
  444.1 1.9 convolution_subtract_fusion
  446.0 0.8 fusion.29
  446.9 2.5 convolution_subtract_fusion.1
  449.4 0.8 fusion.28
  450.2 1.3 fusion.15
  (55 shorter events, 5.0 us)
Async XLA Ops:
  6.5 1.6 copy-start
  6.5 90.9 %reduce-scatter.2.cloned.1.call-start = ((), (), s32[]{:S(2)}) async-start(), calls=%async_computation.1 | async-start | bytes 5242880 | tf_op jit(solution)/shard_map/reduce_scatter | solution.py:20
  17.7 79.8 %copy-start.3 = (s32[1,64]{1,0:T(1,128)S(1)}, s32[1,64]{1,0:T(1,128)}, u32[]{:S(2)}) copy-start(s32[1,64]{1,0:T(1,128)} %param.5) | copy-start | bytes 772
  17.7 134.6 %all-gather.3.cloned.1.call-start = ((), (), s32[]{:S(2)}) async-start(), calls=%async_computation.2 | async-start | bytes 5242880 | tf_op jit(solution)/shard_map/all_gather | solution.py:31
  97.4 130.4 %all-gather.5.cloned.1.call-start = ((), (), s32[]{:S(2)}) async-start(), calls=%async_computation.3 | async-start | bytes 3932160 | tf_op jit(solution)/shard_map/all_gather | solution.py:57
  98.2 61.3 %collective-permute-start = (f32[12]{0:T(128)S(1)}, f32[12]{0:T(128)S(1)}, u32[]{:S(2)}, u32[]{:S(2)}) collective-permute-start(f32[12]{0:T(128)S(1)} %fusion.9), channel_id=1, source_target_pairs={{0,16},{16,0},{1,17},{17,1},{2,18},{18,2},{3,19},{19,3},{4,20},{20... | collective-permute-start | bytes 152 | tf_op jit(solution)/shard_map/ppermute | solution.py:11
  157.1 2.4 collective-permute-start.1
  164.1 124.4 %all-reduce.3.cloned.1.call-start = ((), (), s32[]{:S(2)}) async-start(), calls=%async_computation.4 | async-start | bytes 2097152 | tf_op jit(solution)/shard_map/psum | solution.py:61
  288.5 3.0 collective-permute-start.2
  296.1 1.0 copy-start.2
  439.1 5.0 %copy-start.1 = (f32[512,1536]{1,0:T(8,128)S(1)}, f32[512,1536]{1,0:T(8,128)}, u32[]{:S(2)}) copy-start(f32[512,1536]{1,0:T(8,128)} %all-gather.5.cloned.1.call-done) | copy-start | bytes 9437188
Sparse Core Ops, SparseCore 0:
  17.9 79.5 reduce-scatter.1
  99.3 53.0 all-gather.2
  164.2 63.5 all-gather.4
  237.4 51.0 all-reduce.2
where the time goes:
time: 466 us; the launch traced here: 458 us
  waiting for transfers between devices  251 us (54%)
  other arithmetic  125 us (27%)
  matrix products  40.5 us (9%)
  local copies, waits for them, and re-layouts  24.8 us (5%)
  between operations  16.1 us (3%)
    reduce_scatter x1, waiting for transfers between devices, shards(): lax.psum_scatter(lax.dot_general(sketch, child_blocks, (((0,), (1,)), (()...  79.6 us
    another operation x14, other arithmetic, shards(): lower = jnp.linalg.cholesky(gram)  78.9 us
    all_gather x1, waiting for transfers between devices, shards(): columns_all = lax.all_gather(share, 'col', axis=0, tiled=True)  63.5 us
    all_gather x1, waiting for transfers between devices, shards(): rows_all = lax.all_gather(sketch_part, 'row', axis=1, tiled=True)  53.9 us
    psum x1, waiting for transfers between devices, shards(): gram = lax.psum(gram, 'row')  51.2 us
    another operation x4, other arithmetic, shards(): basis = jax.scipy.linalg.solve_triangular(lower, columns_all, lower=True)  42.5 us
    another operation x12, local copies, waits for them, and re-layouts  13.8 us
    another operation x7, matrix products, shards(): basis = jax.scipy.linalg.solve_triangular(lower, columns_all, lower=True)  11 us
  transfers between devices with their start and end apart: 7, of which 5 were waited for; matrix products, arithmetic and copies ran while one was open for 2% of the time, Pallas kernels for 0%

commit v1 on v0

--- a/solution.py
+++ b/solution.py
@@ -5,6 +5,34 @@
 
 P_SIZE = 12288
 BLK = 128
+
+
+def number_the_ports(u_in, pos_dim):
+    known = list(u_in.shape[1:])
+    known[pos_dim] *= u_in.shape[0]
+    b_now = jnp.moveaxis(u_in, 0, pos_dim).reshape(known)
+    return b_now
+
+
+def assign_the_fields(array_in, mesh_ax, axis_no=1):
+    axis_len = lax.axis_size(mesh_ax)
+    stack_in = tuple(((s, (s + 1) % axis_len) for s in range(axis_len)))
+    e_now, last = ([], [])
+    history = tuple(((tick, m) for m, tick in stack_in))
+    for t in tuple(range(axis_len - 1)):
+        if t % 2 == 0:
+            y = lax.ppermute(e_now[-1] if e_now else array_in, axis_name=mesh_ax, perm=stack_in)
+            e_now.append(y)
+        else:
+            later = lax.ppermute(last[-1] if last else array_in, axis_name=mesh_ax, perm=history)
+            last.append(later)
+    mat_out = jnp.stack([*e_now[::-1], array_in, *last])
+    arr_next = len(e_now)
+    extra = lax.axis_index(mesh_ax)
+    heard = extra - arr_next
+    mat_out = mat_out[(jnp.arange(axis_len) - heard) % axis_len]
+    response = number_the_ports(mat_out, axis_no)
+    return response
 
 
 def from_partner(array, axis, stride):
@@ -28,7 +56,7 @@
     width_here = sketch_part.shape[0]
     parent_blocks = P_SIZE // BLK
     share_blocks = parent_blocks // (siblings * row_count)
-    rows_all = lax.all_gather(sketch_part, "row", axis=1, tiled=True)
+    rows_all = assign_the_fields(sketch_part, "row")
     maps_all = block_map[0]
     block_count = maps_all.shape[0]
     capacity = min(share_blocks, block_count)

time: 466 us -> 502 us (1.077)
  waiting for transfers between devices: 251 us -> 264 us
  local copies, waits for them, and re-layouts: 24.8 us -> 37.6 us
    ppermute x0 -> x3, waiting for transfers between devices: none -> 66.3 us  [the longest x2 44.8 us: assign_the_fields(): lax.ppermute(e_now[-1] if e_now else array_in, axis_name=mesh_ax, perm=st...]
    all_gather x1 -> x0, waiting for transfers between devices: 53.9 us -> none  [shards(): rows_all = lax.all_gather(sketch_part, 'row', axis=1, tiled=True)]
    another operation x12 -> x13, local copies, waits for them, and re-layouts: 13.8 us -> 19.2 us
    transpose x0 -> x1, local copies, waits for them, and re-layouts: none -> 5.34 us  [number_the_ports(): b_now = jnp.moveaxis(u_in, 0, pos_dim).reshape(known)]
  transfers between devices with their start and end apart: 7 -> 9, of which waited for: 5 -> 7; matrix products, arithmetic and copies ran while one was open for 2% -> 6% of each run, Pallas kernels for 0% -> 0%
where the time goes in v1:
time: 502 us; the launch traced here: 493 us
  waiting for transfers between devices  264 us (53%)
  other arithmetic  129 us (26%)
  matrix products  42.7 us (9%)
  local copies, waits for them, and re-layouts  37.6 us (7%)
  between operations  16 us (3%)
    reduce_scatter x1, waiting for transfers between devices, shards(): lax.psum_scatter(lax.dot_general(sketch, child_blocks, (((0,), (1,)), (()...  79.6 us
    another operation x14, other arithmetic, shards(): lower = jnp.linalg.cholesky(gram)  78.9 us
    all_gather x1, waiting for transfers between devices, shards(): columns_all = lax.all_gather(share, 'col', axis=0, tiled=True)  63.4 us
    psum x1, waiting for transfers between devices, shards(): gram = lax.psum(gram, 'row')  51.3 us
    ppermute x2, waiting for transfers between devices, assign_the_fields(): lax.ppermute(e_now[-1] if e_now else array_in, axis_name=mesh_ax, perm=st...  44.8 us
    another operation x4, other arithmetic, shards(): basis = jax.scipy.linalg.solve_triangular(lower, columns_all, lower=True)  42.5 us
    ppermute x1, waiting for transfers between devices, assign_the_fields(): lax.ppermute(last[-1] if last else array_in, axis_name=mesh_ax, perm=hist...  21.5 us
    another operation x12, local copies, waits for them, and re-layouts  13.8 us
  transfers between devices with their start and end apart: 9, of which 7 were waited for; matrix products, arithmetic and copies ran while one was open for 6% of the time, Pallas kernels for 0%

profile of v1, /device:TPU:0, one launch (start us, length us, event | category | flops | bytes accessed | tf_op | source)
XLA Modules:
  0.0 493.2 jit_solution(11993610545763506369)
XLA Ops:
  6.5 1.6 copy-done
  8.1 9.6 %fusion.82 = f32[512,2048]{1,0:T(8,128)} fusion(bf16[2048,512]{1,0:T(8,128)(2,1)S(1)} %copy-done, bf16[2048,2048]{1,0:T(8,128)(2,1)} %param.3), kind=kOutput, calls=%fused_computation.150 | convolution fusion | flops 4294967296 | bytes 14680064 | tf_op jit(solution)/shard_map/dot_general | solution.py:49
  17.8 79.6 %reduce-scatter.2.cloned.1.call-done = f32[128,2048]{1,0:T(8,128)} async-done(((f32[512,2048]{1,0:T(8,128)}), f32[128,2048]{1,0:T(8,128)}) %reduce-scatter.2.cloned.1.call-update) | async-done | bytes 1048592 | tf_op jit(solution)/shard_map/reduce_scatter | solution.py:48
  97.4 1.5 collective-permute-start
  99.3 1.5 collective-permute-start.2
  100.8 23.8 %collective-permute-done = f32[128,2048]{1,0:T(8,128)S(1)} collective-permute-done((f32[128,2048]{1,0:T(8,128)}, f32[128,2048]{1,0:T(8,128)S(1)}, u32[]{:S(2)}, u32[]{:S(2)}) %collective-permute-start) | collective-permute-done | bytes 1048608 | tf_op jit(solution)/shard_map/ppermute | solution.py:24
  125.7 21.5 %collective-permute-done.2 = f32[128,2048]{1,0:T(8,128)} collective-permute-done((f32[128,2048]{1,0:T(8,128)}, f32[128,2048]{1,0:T(8,128)}, u32[]{:S(2)}, u32[]{:S(2)}) %collective-permute-start.2) | collective-permute-done | bytes 1048608 | tf_op jit(solution)/shard_map/ppermute | solution.py:27
  147.2 21.0 %collective-permute-done.1 = f32[128,2048]{1,0:T(8,128)} collective-permute-done((f32[128,2048]{1,0:T(8,128)S(1)}, f32[128,2048]{1,0:T(8,128)}, u32[]{:S(2)}, u32[]{:S(2)}) %collective-permute-start.1) | collective-permute-done | bytes 1048608 | tf_op jit(solution)/shard_map/ppermute | solution.py:24
  168.2 4.2 pad_maximum_fusion
  172.4 5.0 %gather_fusion = f32[4,128,2048]{2,1,0:T(8,128)} fusion(f32[4,128,2048]{2,1,0:T(8,128)} %pad_maximum_fusion, s32[1024]{0:T(1024)S(1)} %pad_clamp_fusion), kind=kCustom, calls=%fused_computation | custom fusion | bytes 8388624 | tf_op jit(solution)/shard_map/gather | solution.py:33
  177.3 5.3 %copy.19 = f32[128,4,2048]{0,2,1:T(8,128)} copy(f32[128,4,2048]{2,0,1:T(8,128)} %bitcast.112) | data formatting | bytes 8388608 | tf_op jit(solution)/shard_map/transpose | solution.py:13
  182.7 5.4 %copy.20 = f32[128,64,128]{2,1,0:T(8,128)} copy(f32[128,64,128]{0,2,1:T(8,128)} %bitcast.113) | data formatting | bytes 8388608 | tf_op jit(solution)/shard_map/reshape;reshape | solution.py:63
  188.1 3.8 convolution_bitcast_fusion
  192.4 1.6 convolution_bitcast_fusion.1
  194.6 1.0 fusion.8
  195.6 1.2 copy.24
  196.9 2.3 copy.25
  199.4 63.4 %all-gather.2.cloned.1.call-done = f32[512,1536]{1,0:T(8,128)} async-done(((f32[128,1536]{1,0:T(8,128)}), f32[512,1536]{1,0:T(8,128)}) %all-gather.2.cloned.1.call-update) | async-done | bytes 3145744 | tf_op jit(solution)/shard_map/all_gather | solution.py:85
  262.8 9.4 %fusion.83 = f32[512,512]{0,1:T(8,128)} fusion(f32[512,1536]{1,0:T(8,128)} %all-gather.2.cloned.1.call-done), kind=kOutput, calls=%fused_computation.151 | convolution fusion | flops 4831838208 | bytes 4194304 | tf_op jit(solution)/shard_map/dot_general | solution.py:86
  272.2 51.3 %all-reduce.3.cloned.1.call-done = f32[512,512]{0,1:T(8,128)} async-done(((f32[512,512]{0,1:T(8,128)}), f32[512,512]{0,1:T(8,128)}) %all-reduce.3.cloned.1.call-update) | async-done | bytes 1048592 | tf_op jit(solution)/shard_map/psum | solution.py:89
  323.5 3.0 collective-permute-done.5
  326.5 1.7 add.176
  328.2 1.3 copy.27
  329.6 1.4 fusion.11
  331.0 1.0 copy-done.3
  332.0 11.7 %cholesky.104 = f32[128,128]{1,0:T(8,128)S(1)} custom-call(f32[128,128]{1,0:T(8,128)S(1)} %cholesky.266), custom_call_target="Cholesky" | custom-call | tf_op jit(solution)/shard_map/jit(cholesky)/cholesky | solution.py:92
  343.9 9.8 %custom-call.31 = f32[1,128,128]{1,2,0:T(8,128)S(1)} custom-call(f32[1,128,128]{2,1,0:T(8,128)S(1)} %get-tuple-element.38), custom_call_target="InvertDiagBlocksLowerTriangular" | custom-call | tf_op jit(solution)/shard_map/jit(cholesky)/cholesky | solution.py:92
  353.7 1.2 constant_dynamic-update-slice_fusion
  354.9 1.3 slice_subtract_fusion
  356.2 11.7 %cholesky.217 = f32[128,128]{1,0:T(8,128)S(1)} custom-call(f32[128,128]{1,0:T(8,128)S(1)} %cholesky.270), custom_call_target="Cholesky" | custom-call | tf_op jit(solution)/shard_map/jit(cholesky)/cholesky | solution.py:92
  368.0 10.2 %custom-call.32 = f32[1,128,128]{1,2,0:T(8,128)S(1)} custom-call(f32[1,128,128]{2,1,0:T(8,128)S(1)} %get-tuple-element.35), custom_call_target="InvertDiagBlocksLowerTriangular" | custom-call | tf_op jit(solution)/shard_map/jit(cholesky)/cholesky | solution.py:92
  378.4 1.3 slice_subtract_fusion.1
  379.7 11.7 %cholesky.238 = f32[128,128]{1,0:T(8,128)S(1)} custom-call(f32[128,128]{1,0:T(8,128)S(1)} %cholesky.275), custom_call_target="Cholesky" | custom-call | tf_op jit(solution)/shard_map/jit(cholesky)/cholesky | solution.py:92
  391.5 9.8 %custom-call.33 = f32[1,128,128]{1,2,0:T(8,128)S(1)} custom-call(f32[1,128,128]{2,1,0:T(8,128)S(1)} %get-tuple-element.32), custom_call_target="InvertDiagBlocksLowerTriangular" | custom-call | tf_op jit(solution)/shard_map/jit(cholesky)/cholesky | solution.py:92
  401.5 1.2 slice_subtract_fusion.2
  402.7 11.9 %cholesky.255 = f32[128,128]{1,0:T(8,128)S(1)} custom-call(f32[128,128]{1,0:T(8,128)S(1)} %slice_subtract_fusion.2), custom_call_target="Cholesky" | custom-call | tf_op jit(solution)/shard_map/jit(cholesky)/cholesky | solution.py:92
  419.0 1.1 select_select_fusion
  420.1 13.8 %while.1 = (s32[]{:T(128)}, f32[512,512]{1,0:T(8,128)}, s32[4,2]{0,1:T(2,128)S(1)}, f32[4,128,128]{2,1,0:T(8,128)}, s32[]{:T(128)}) while((s32[]{:T(128)}, f32[512,512]{1,0:T(8,128)}, s32[4,2]{0,1:T(2,128)S(1)}, f32[4,128,128]{2,1,0:T(8,128)}, s32[]{:T(128)}) %tuple.31), condition=%wide.while_cond, body=%wide.while_body.sunk | while | flops 2 | bytes 132205 | solution.py:93
  420.7 2.9 bitcast_dynamic-update-slice_fusion.2
  424.2 2.9 bitcast_dynamic-update-slice_fusion.2
  427.7 2.9 bitcast_dynamic-update-slice_fusion.2
  431.2 2.8 bitcast_dynamic-update-slice_fusion.2
  434.0 40.1 %custom-call.34 = f32[4,128,128]{1,2,0:T(8,128)S(1)} custom-call(f32[4,128,128]{2,1,0:T(8,128)} %get-tuple-element.12), custom_call_target="InvertDiagBlocksLowerTriangular" | custom-call | tf_op jit(solution)/shard_map/jit(_solve_triangular)/triangular_solve | solution.py:93
  474.1 2.1 fusion.16
  476.2 2.0 convolution_subtract_fusion.2
  479.0 1.9 convolution_subtract_fusion
  481.8 2.5 convolution_subtract_fusion.1
  485.2 1.3 fusion.15
  (65 shorter events, 10.6 us)
Async XLA Ops:
  6.5 1.6 copy-start
  6.5 90.9 %reduce-scatter.2.cloned.1.call-start = ((), (), s32[]{:S(2)}) async-start(), calls=%async_computation.1 | async-start | bytes 5242880 | tf_op jit(solution)/shard_map/reduce_scatter | solution.py:48
  17.7 81.2 %copy-start.4 = (s32[1,64]{1,0:T(1,128)S(1)}, s32[1,64]{1,0:T(1,128)}, u32[]{:S(2)}) copy-start(s32[1,64]{1,0:T(1,128)} %param.5) | copy-start | bytes 772
  17.7 245.0 %all-gather.2.cloned.1.call-start = ((), (), s32[]{:S(2)}) async-start(), calls=%async_computation.2 | async-start | bytes 3932160 | tf_op jit(solution)/shard_map/all_gather | solution.py:85
  97.4 27.1 %collective-permute-start = (f32[128,2048]{1,0:T(8,128)}, f32[128,2048]{1,0:T(8,128)S(1)}, u32[]{:S(2)}, u32[]{:S(2)}) collective-permute-start(f32[128,2048]{1,0:T(8,128)} %reduce-scatter.2.cloned.1.call-done), channel_id=1, source_target_pairs={{0,4},{4,8},{8,12},{12,0},{1,5},{5,9},{9,13},{13,1},{2,6},{6,10},{... | collective-permute-start | bytes 3145736 | tf_op jit(solution)/shard_map/ppermute | solution.py:24
  99.3 47.9 %collective-permute-start.2 = (f32[128,2048]{1,0:T(8,128)}, f32[128,2048]{1,0:T(8,128)}, u32[]{:S(2)}, u32[]{:S(2)}) collective-permute-start(f32[128,2048]{1,0:T(8,128)} %reduce-scatter.2.cloned.1.call-done), channel_id=1, source_target_pairs={{4,0},{8,4},{12,8},{0,12},{5,1},{9,5},{13,9},{1,13},{6,2},{10,6},{... | collective-permute-start | bytes 3145736 | tf_op jit(solution)/shard_map/ppermute | solution.py:27
  124.6 43.6 %collective-permute-start.1 = (f32[128,2048]{1,0:T(8,128)S(1)}, f32[128,2048]{1,0:T(8,128)}, u32[]{:S(2)}, u32[]{:S(2)}) collective-permute-start(f32[128,2048]{1,0:T(8,128)S(1)} %collective-permute-done), channel_id=1, source_target_pairs={{0,4},{4,8},{8,12},{12,0},{1,5},{5,9},{9,13},{13,1},{2,6},{6,10},{... | collective-permute-start | bytes 3145736 | tf_op jit(solution)/shard_map/ppermute | solution.py:24
  125.4 69.2 %collective-permute-start.3 = (f32[12]{0:T(128)S(1)}, f32[12]{0:T(128)S(1)}, u32[]{:S(2)}, u32[]{:S(2)}) collective-permute-start(f32[12]{0:T(128)S(1)} %fusion.9), channel_id=1, source_target_pairs={{0,16},{16,0},{1,17},{17,1},{2,18},{18,2},{3,19},{19,3},{4,20},{20... | collective-permute-start | bytes 152 | tf_op jit(solution)/shard_map/ppermute | solution.py:39
  188.1 4.3 copy-start.1
  192.2 2.4 collective-permute-start.4
  199.2 124.3 %all-reduce.3.cloned.1.call-start = ((), (), s32[]{:S(2)}) async-start(), calls=%async_computation.3 | async-start | bytes 2097152 | tf_op jit(solution)/shard_map/psum | solution.py:89
  323.5 3.0 collective-permute-start.5
  331.0 1.0 copy-start.3
  474.1 5.0 %copy-start.2 = (f32[512,1536]{1,0:T(8,128)S(1)}, f32[512,1536]{1,0:T(8,128)}, u32[]{:S(2)}) copy-start(f32[512,1536]{1,0:T(8,128)} %all-gather.2.cloned.1.call-done) | copy-start | bytes 9437188
Sparse Core Ops, SparseCore 0:
  17.9 79.5 reduce-scatter.1
  199.3 63.4 all-gather.1
  272.3 51.0 all-reduce.2
